TPU v7x, 32 devices: a whole 2x2x4 slice. The times are simulated.
32 devices in a mesh: group: 2 (over y), shard: 16 (over z, x, core).
Axes of the slice: x: 2, y: 2, z: 4, core: 2. Of those that a mesh axis runs over, the one named last changes fastest.
Arguments:
- samples: bfloat16 [32, 8192], P('shard'), may hold values from -6 to 6
- factor_old: float32 [8192, 8192], P('shard', 'group'), as said below
- damping: float32 [1], replicated, may hold values from 0.1 to 1
- gradients: bfloat16 [2048, 8192], P('shard', 'group'), may hold values from -6 to 6
Outputs:
- swept_factor: float32 [8192, 8192], P('shard', 'group')
- update: bfloat16 [8192, 2048], P('shard', 'group')
Inputs may be any that keep to these rules, and one draw needn't show every extreme that they name: factor_old is symmetric and positive definite.
All inputs are finite; a program needn't handle non-finite values.
Results may differ from a plain program's by a relative error of at most 0.0049.
Values may be sent and summed in bfloat16 or wider, within the bound.
A program may use at most 128 MiB of HBM per device.

v0:
```python
import jax
import jax.numpy as jnp
from jax import lax
from jax.sharding import PartitionSpec as P

D = 8192
BLOCK = 128
PIVOTS = 2
ema_keep = 0.5


def spread(block, axis, holder):
    block = jnp.where(lax.axis_index(axis) == holder, block, jnp.zeros_like(block))
    return lax.psum(block, axis)


def solve_spd(pivot_block, right_side):
    lower_factor = jnp.linalg.cholesky(pivot_block)
    half_solved = lax.linalg.triangular_solve(lower_factor, right_side, left_side=True, lower=True)
    return lax.linalg.triangular_solve(
        lower_factor, half_solved, left_side=True, lower=True, transpose_a=True
    )


def on_device(samples, factor_old, damping, gradients):
    row_count, col_count = factor_old.shape
    shard_index = lax.axis_index("shard")
    group_index = lax.axis_index("group")
    row_first = shard_index * row_count
    col_first = group_index * col_count
    total_tokens = samples.shape[0] * lax.axis_size("shard")
    contract = (((0,), (0,)), ((), ()))
    token_piece = lax.all_gather(samples, "shard", axis=0, tiled=True)
    left_part = lax.dynamic_slice_in_dim(token_piece, row_first, row_count, 1)
    right_part = lax.dynamic_slice_in_dim(token_piece, col_first, col_count, 1)
    covariance = lax.dot_general(
        left_part, right_part, contract, preferred_element_type=jnp.float32
    )
    row_ids = lax.broadcasted_iota(jnp.int32, (row_count, col_count), 0) + row_first
    col_ids = lax.broadcasted_iota(jnp.int32, (row_count, col_count), 1) + col_first
    diagonal = jnp.where(row_ids == col_ids, damping[0], 0.0)
    factor = ema_keep * factor_old + (1.0 - ema_keep) * (covariance / total_tokens) + diagonal
    spacing = D // PIVOTS
    sel_rows = lax.broadcasted_iota(jnp.int32, (BLOCK, col_count), 0)
    sel_cols = lax.broadcasted_iota(jnp.int32, (BLOCK, col_count), 1) + col_first

    def sweep_once(sweep_step, matrix):
        first_index = (sweep_step * spacing).astype(jnp.int32)
        col_owner = first_index // col_count
        row_owner = first_index // row_count
        col_offset = first_index - col_owner * col_count
        row_offset = first_index - row_owner * row_count
        own_columns = lax.dynamic_slice_in_dim(matrix, col_offset, BLOCK, 1)
        column = spread(own_columns, "group", col_owner)
        own_rows = lax.dynamic_slice_in_dim(matrix, row_offset, BLOCK, 0)
        own_pivot = lax.dynamic_slice_in_dim(column, row_offset, BLOCK, 0)
        pivot_strip, pivot_block = (
            spread(own_rows, "shard", row_owner),
            spread(own_pivot, "shard", row_owner),
        )
        selector = jnp.where(sel_cols == sel_rows + first_index, 1.0, 0.0).astype(jnp.float32)
        factor_q = solve_spd(pivot_block, pivot_strip + selector)
        matrix = matrix - jnp.dot(
            column, factor_q, precision=lax.Precision.HIGHEST, preferred_element_type=jnp.float32
        )
        addition = jnp.where(shard_index == row_owner, factor_q, 0.0)
        block_rows = lax.dynamic_slice_in_dim(matrix, row_offset, BLOCK, 0) + addition
        return lax.dynamic_update_slice_in_dim(matrix, block_rows, row_offset, 0)

    swept_factor = lax.fori_loop(0, PIVOTS, sweep_once, factor)
    swept_half = swept_factor.astype(jnp.bfloat16)
    partial_terms = lax.dot_general(
        swept_half,
        lax.all_gather(gradients, "shard", axis=0, tiled=True),
        (((1,), (1,)), ((), ())),
        preferred_element_type=jnp.float32,
    )
    update = lax.psum_scatter(partial_terms, "group", scatter_dimension=1, tiled=True).astype(
        jnp.bfloat16
    )
    return (swept_factor, update)


def solution(mesh):
    return jax.shard_map(
        on_device,
        mesh=mesh,
        in_specs=(P("shard", None), P("shard", "group"), P(), P("shard", "group")),
        out_specs=(P("shard", "group"), P("shard", "group")),
        check_vma=False,
    )
```

profile of v0, /device:TPU:0, one launch (start us, length us, event | category | flops | bytes accessed | tf_op | source)
XLA Modules:
  0.0 591.6 jit_solution(10280611587841758913)
XLA Ops:
  8.0 24.8 %all-gather = bf16[16,2,8192]{2,1,0:T(2,128)(2,1)S(1)} all-gather(bf16[1,2,8192]{2,1,0:T(2,128)(2,1)} %bitcast.32), channel_id=1, replica_groups=mesh['group'=2,'shard'=16] {'shard'}, dimensions={0}, use_global_device_ids=true | all-gather | bytes 557056 | tf_op jit(solution)/shard_map/all_gather | solution.py:33
  32.9 0.2 reshape.41
  33.7 6.7 %select_add_fusion = f32[512,4096]{1,0:T(8,128)} fusion(f32[512,4096]{1,0:T(8,128)} %param.7, f32[]{:T(128)} %bitcast.31, s32[4096]{0:T(1024)S(1)} %iota_add_fusion.1, s32[512]{0:T(512)S(1)} %iota_add_fusion.2, bf16[32,8192]{1,0:T(8,128)(2,1)S(1)} %reshape.41, s32[]{:T(128)S(6)} %select_n.180, s32[]{:T(128)S(6)} %select_n.179), kind=kOutput, calls=%fused_computation.29 | convolution fusion | flops 146800640 | bytes 17090572 | tf_op jit(solution)/shard_map/dot_general | solution.py:36
  40.4 345.1 %while.17 = (s32[]{:T(128)}, f32[512,4096]{1,0:T(8,128)}, s32[]{:T(128)}, s32[4096]{0:T(1024)S(1)}, s32[]{:T(128)}, /*index=5*/s32[]{:T(128)}, s32[]{:T(128)}, s...) while((s32[]{:T(128)}, f32[512,4096]{1,0:T(8,128)}, ...), condition=%wide.region_6.7_spmd.clone, body=%wide.region_0.6_spmd.clone.sunk | while | flops 4838440960 | bytes 54937316 | solution.py:70
  40.4 1.7 dynamic-slice_select_fusion.6
  42.0 0.0 all-reduce.6.cloned.1.call-update
  42.1 0.0 all-reduce.8.cloned.1.call-start
  42.2 3.1 dynamic-slice_select_fusion.7
  45.3 19.4 %all-reduce.6.cloned.1.call-done = f32[512,128]{1,0:T(8,128)} async-done(((f32[512,128]{1,0:T(8,128)}), f32[512,128]{1,0:T(8,128)}) %all-reduce.6.cloned.1.call-update) | async-done | bytes 262160 | tf_op jit(solution)/shard_map/while/body/eval_jaxpr/psum | solution.py:14
  64.6 1.5 dynamic-slice_select_fusion.8
  66.1 0.0 all-reduce.8.cloned.1.call-update
  66.1 101.6 %all-reduce.8.cloned.1.call-done = (f32[128,4096]{1,0:T(8,128)}, f32[128,128]{1,0:T(8,128)}) async-done(((f32[128,4096]{1,0:T(8,128)}, f32[128,128]{1,0:T(8,128)}), (f32[128,4096]{1,0:T(8,128)}, f32[128,128]{1,0:T(8,128)})) %all-reduce.8.cloned.1.call-update) | async-done | bytes 2162704 | tf_op jit(solution)/shard_map/while/body/eval_jaxpr/psum | solution.py:14
  167.7 0.9 copy.9
  168.6 0.9 fusion.45
  169.5 11.7 %cholesky.59 = f32[128,128]{1,0:T(8,128)S(1)} custom-call(f32[128,128]{1,0:T(8,128)S(1)} %fusion.45), custom_call_target="Cholesky" | custom-call | tf_op jit(solution)/shard_map/while/body/eval_jaxpr/jit(cholesky)/cholesky | solution.py:18
  181.2 0.6 compare_reduce_fusion.2
  181.9 0.7 fusion.46
  182.6 9.8 %custom-call.26 = f32[1,128,128]{1,2,0:T(8,128)S(1)} custom-call(f32[1,128,128]{2,1,0:T(8,128)S(1)} %fusion.46), custom_call_target="InvertDiagBlocksLowerTriangular" | custom-call | tf_op jit(solution)/shard_map/while/body/eval_jaxpr/triangular_solve | solution.py:20
  192.4 3.6 fusion.47
  196.0 1.9 fusion.48
  197.9 11.1 %convolution_subtract_fusion.2 = f32[512,4096]{1,0:T(8,128)} fusion(f32[512,4096]{1,0:T(8,128)} %get-tuple-element.225, f32[512,128]{1,0:T(8,128)S(1)} %copy-done, f32[128,4096]{1,0:T(8,128)S(1)} %fusion.48), kind=kOutput, calls=%fused_computation.2.clone.1 | convolution fusion | flops 3223322624 | bytes 19136512 | tf_op jit(solution)/shard_map/while/body/eval_jaxpr/dot_general | solution.py:63
  209.1 3.2 add_dynamic-update-slice_fusion.2
  212.3 0.0 all-reduce.6.cloned.1.call-start
  212.3 1.7 dynamic-slice_select_fusion.6
  213.9 0.0 all-reduce.6.cloned.1.call-update
  214.0 0.0 all-reduce.8.cloned.1.call-start
  214.1 3.1 dynamic-slice_select_fusion.7
  217.2 20.8 %all-reduce.6.cloned.1.call-done = f32[512,128]{1,0:T(8,128)} async-done(((f32[512,128]{1,0:T(8,128)}), f32[512,128]{1,0:T(8,128)}) %all-reduce.6.cloned.1.call-update) | async-done | bytes 262160 | tf_op jit(solution)/shard_map/while/body/eval_jaxpr/psum | solution.py:14
  237.9 1.5 dynamic-slice_select_fusion.8
  239.4 0.0 all-reduce.8.cloned.1.call-update
  239.4 101.5 %all-reduce.8.cloned.1.call-done = (f32[128,4096]{1,0:T(8,128)}, f32[128,128]{1,0:T(8,128)}) async-done(((f32[128,4096]{1,0:T(8,128)}, f32[128,128]{1,0:T(8,128)}), (f32[128,4096]{1,0:T(8,128)}, f32[128,128]{1,0:T(8,128)})) %all-reduce.8.cloned.1.call-update) | async-done | bytes 2162704 | tf_op jit(solution)/shard_map/while/body/eval_jaxpr/psum | solution.py:14
  340.9 0.9 copy.9
  341.8 0.9 fusion.45
  342.7 11.7 %cholesky.59 = f32[128,128]{1,0:T(8,128)S(1)} custom-call(f32[128,128]{1,0:T(8,128)S(1)} %fusion.45), custom_call_target="Cholesky" | custom-call | tf_op jit(solution)/shard_map/while/body/eval_jaxpr/jit(cholesky)/cholesky | solution.py:18
  354.4 0.6 compare_reduce_fusion.2
  355.1 0.7 fusion.46
  355.7 9.8 %custom-call.26 = f32[1,128,128]{1,2,0:T(8,128)S(1)} custom-call(f32[1,128,128]{2,1,0:T(8,128)S(1)} %fusion.46), custom_call_target="InvertDiagBlocksLowerTriangular" | custom-call | tf_op jit(solution)/shard_map/while/body/eval_jaxpr/triangular_solve | solution.py:20
  365.6 3.6 fusion.47
  369.2 1.9 fusion.48
  371.1 11.1 %convolution_subtract_fusion.2 = f32[512,4096]{1,0:T(8,128)} fusion(f32[512,4096]{1,0:T(8,128)} %get-tuple-element.225, f32[512,128]{1,0:T(8,128)S(1)} %copy-done, f32[128,4096]{1,0:T(8,128)S(1)} %fusion.48), kind=kOutput, calls=%fused_computation.2.clone.1 | convolution fusion | flops 3223322624 | bytes 19136512 | tf_op jit(solution)/shard_map/while/body/eval_jaxpr/dot_general | solution.py:63
  382.2 3.2 add_dynamic-update-slice_fusion.2
  385.5 0.6 all-gather.3.cloned.1.call-update
  386.0 0.0 reduce-scatter.2.cloned.1.call-start
  386.1 126.8 %all-gather.3.cloned.1.call-done = bf16[2048,4096]{1,0:T(8,128)(2,1)} async-done(((bf16[128,4096]{1,0:T(8,128)(2,1)}), bf16[2048,4096]{1,0:T(8,128)(2,1)}) %all-gather.3.cloned.1.call-update) | async-done | bytes 16777232 | tf_op jit(solution)/shard_map/all_gather | solution.py:74
  512.9 16.2 %fusion.20 = f32[512,2048]{1,0:T(8,128)} fusion(bf16[2048,4096]{1,0:T(8,128)(2,1)} %all-gather.3.cloned.1.call-done, f32[512,4096]{1,0:T(8,128)} %get-tuple-element.154), kind=kOutput, calls=%fused_computation.30 | convolution fusion | flops 8592031744 | bytes 29360128 | tf_op jit(solution)/shard_map/dot_general | solution.py:72
  529.1 0.0 reduce-scatter.2.cloned.1.call-update
  529.1 52.6 %reduce-scatter.2.cloned.1.call-done = f32[512,1024]{1,0:T(8,128)} async-done(((f32[512,2048]{1,0:T(8,128)}), f32[512,1024]{1,0:T(8,128)}) %reduce-scatter.2.cloned.1.call-update) | async-done | bytes 2097168 | tf_op jit(solution)/shard_map/reduce_scatter | solution.py:78
  581.7 2.7 convert_element_type.7
  (10 shorter events, 0.1 us)
Async XLA Ops:
  40.4 24.2 %all-reduce.6.cloned.1.call-start = ((), (), s32[]{:S(2)}) async-start(), calls=%async_computation.3 | async-start | bytes 524288 | tf_op jit(solution)/shard_map/while/body/eval_jaxpr/psum | solution.py:14
  42.1 125.6 %all-reduce.8.cloned.1.call-start = ((), (), s32[]{:S(2)}) async-start(), calls=%async_computation.4 | async-start | bytes 4325376 | tf_op jit(solution)/shard_map/while/body/eval_jaxpr/psum | solution.py:14
  192.4 5.6 copy-start
  212.3 25.6 %all-reduce.6.cloned.1.call-start = ((), (), s32[]{:S(2)}) async-start(), calls=%async_computation.3 | async-start | bytes 524288 | tf_op jit(solution)/shard_map/while/body/eval_jaxpr/psum | solution.py:14
  214.0 126.9 %all-reduce.8.cloned.1.call-start = ((), (), s32[]{:S(2)}) async-start(), calls=%async_computation.4 | async-start | bytes 4325376 | tf_op jit(solution)/shard_map/while/body/eval_jaxpr/psum | solution.py:14
  365.6 5.6 copy-start
  385.5 127.5 %all-gather.3.cloned.1.call-start = ((), (), s32[]{:S(2)}) async-start(), calls=%async_computation.1 | async-start | bytes 17825792 | tf_op jit(solution)/shard_map/all_gather | solution.py:74
  386.0 195.7 %reduce-scatter.2.cloned.1.call-start = ((), (), s32[]{:S(2)}) async-start(), calls=%async_computation.2 | async-start | bytes 6291456 | tf_op jit(solution)/shard_map/reduce_scatter | solution.py:78
Sparse Core Ops, SparseCore 0:
  44.0 20.5 all-reduce.5
  68.8 98.8 all-reduce.7
  215.9 21.9 all-reduce.5
  241.9 98.9 all-reduce.7
Sparse Core Ops, SparseCore 1:
  388.1 124.8 all-gather.2
  529.2 52.5 reduce-scatter.1
where the time goes:
time: 592 us
  waiting for transfers between devices  423 us (71%)
  other arithmetic  69.1 us (12%)
  matrix products  56.1 us (9%)
  blocking collectives  24.8 us (4%)
  between operations  15.8 us (3%)
    psum x4, waiting for transfers between devices, spread(): return lax.psum(block, axis)  243 us
    all_gather x1, waiting for transfers between devices, on_device(): lax.all_gather(gradients, 'shard', axis=0, tiled=True)  127 us
    reduce_scatter x1, waiting for transfers between devices, on_device(): lax.psum_scatter(partial_terms, 'group', scatter_dimension=1, tiled=True)  52.6 us
    all_gather x1, blocking collectives, on_device(): token_piece = lax.all_gather(samples, 'shard', axis=0, tiled=True)  24.8 us
    another operation x6, other arithmetic, solve_spd(): lower_factor = jnp.linalg.cholesky(pivot_block)  24.8 us
    dot_general x2, matrix products, sweep_once(): jnp.dot(column, factor_q, precision=lax.Precision.HIGHEST, preferred_elem...  22.2 us
    another operation x4, other arithmetic, solve_spd(): lax.linalg.triangular_solve(lower_factor, half_solved, left_side=True, lo...  20.9 us
    dot_general x1, matrix products, on_device(): lax.dot_general(swept_half, lax.all_gather(gradients, 'shard', axis=0, ti...  16.2 us
  transfers between devices with their start and end apart: 6, of which 6 were waited for; matrix products, arithmetic and copies ran while one was open for 1% of the time, Pallas kernels for 0%

commit v1 on v0

--- a/solution.py
+++ b/solution.py
@@ -7,6 +7,18 @@
 BLOCK = 128
 PIVOTS = 2
 ema_keep = 0.5
+
+
+def doubled_up(value, axis, dim):
+    ways, here = (lax.axis_size(axis), lax.axis_index(axis))
+    grown, reach = (value, 1)
+    while reach < ways:
+        theirs = lax.ppermute(grown, axis, [(d, d ^ reach) for d in range(ways)])
+        mine_first = jnp.concatenate([grown, theirs], axis=dim)
+        theirs_first = jnp.concatenate([theirs, grown], axis=dim)
+        grown = jnp.where(here & reach == 0, mine_first, theirs_first)
+        reach = 2 * reach
+    return grown
 
 
 def spread(block, axis, holder):
@@ -71,7 +83,7 @@
     swept_half = swept_factor.astype(jnp.bfloat16)
     partial_terms = lax.dot_general(
         swept_half,
-        lax.all_gather(gradients, "shard", axis=0, tiled=True),
+        doubled_up(gradients, "shard", 0),
         (((1,), (1,)), ((), ())),
         preferred_element_type=jnp.float32,
     )

time: 592 us -> 914 us (1.54)
  waiting for transfers between devices: 423 us -> 643 us
  blocking collectives: 24.8 us -> 106 us
  other arithmetic: 69.1 us -> 82.9 us
    psum x4, waiting for transfers between devices: 243 us -> 542 us  [spread(): return lax.psum(block, axis)]
    all_gather x1 -> x0, waiting for transfers between devices: 127 us -> none  [on_device(): lax.all_gather(gradients, 'shard', axis=0, tiled=True)]
    all_gather x1, blocking collectives: 24.8 us -> 106 us  [on_device(): token_piece = lax.all_gather(samples, 'shard', axis=0, tiled=True)]
    ppermute x0 -> x4, waiting for transfers between devices: none -> 48.5 us  [doubled_up(): theirs = lax.ppermute(grown, axis, [(d, d ^ reach) for d in range(ways)])]
    select_n x0 -> x3, other arithmetic: none -> 19.3 us  [doubled_up(): grown = jnp.where(here & reach == 0, mine_first, theirs_first)]
  transfers between devices with their start and end apart: 6 -> 9, of which waited for: 6 -> 7; matrix products, arithmetic and copies ran while one was open for 1% -> 10% of each run, Pallas kernels for 0% -> 0%
where the time goes in v1:
time: 914 us; the launch traced here: 913 us
  waiting for transfers between devices  643 us (70%)
  blocking collectives  106 us (12%)
  other arithmetic  82.9 us (9%)
  matrix products  50.6 us (6%)
  between operations  15.9 us (2%)
    psum x4, waiting for transfers between devices, spread(): return lax.psum(block, axis)  542 us
    all_gather x1, blocking collectives, on_device(): token_piece = lax.all_gather(samples, 'shard', axis=0, tiled=True)  106 us
    reduce_scatter x1, waiting for transfers between devices, on_device(): lax.psum_scatter(partial_terms, 'group', scatter_dimension=1, tiled=True)  53.1 us
    ppermute x4, waiting for transfers between devices, doubled_up(): theirs = lax.ppermute(grown, axis, [(d, d ^ reach) for d in range(ways)])  48.5 us
    another operation x6, other arithmetic, solve_spd(): lower_factor = jnp.linalg.cholesky(pivot_block)  24.8 us
    another operation x4, other arithmetic, solve_spd(): lax.linalg.triangular_solve(lower_factor, half_solved, left_side=True, lo...  20.9 us
    select_n x3, other arithmetic, doubled_up(): grown = jnp.where(here & reach == 0, mine_first, theirs_first)  19.3 us
  transfers between devices with their start and end apart: 9, of which 7 were waited for; matrix products, arithmetic and copies ran while one was open for 10% of the time, Pallas kernels for 0%

profile of v1, /device:TPU:0, one launch (start us, length us, event | category | flops | bytes accessed | tf_op | source)
XLA Modules:
  0.0 913.4 jit_solution(1676411638051019)
XLA Ops:
  8.0 0.6 collective-permute-start
  8.6 2.5 collective-permute-done
  11.1 2.3 maximum_select_fusion.4
  13.3 2.9 collective-permute-start.1
  16.3 46.0 %collective-permute-done.1 = bf16[256,4096]{1,0:T(8,128)(2,1)} collective-permute-done((bf16[256,4096]{1,0:T(8,128)(2,1)S(1)}, bf16[256,4096]{1,0:T(8,128)(2,1)}, u32[]{:S(2)}, u32[]{:S(2)}) %collective-permute-start.1) | collective-permute-done | bytes 2097184 | tf_op jit(solution)/shard_map/ppermute | solution.py:16
  62.3 4.7 maximum_select_fusion.3
  67.0 1.8 collective-permute-start.2
  69.4 106.1 %all-gather = bf16[16,2,8192]{2,1,0:T(2,128)(2,1)S(1)} all-gather(bf16[1,2,8192]{2,1,0:T(2,128)(2,1)S(1)} %bitcast.33), channel_id=1, replica_groups=mesh['group'=2,'shard'=16] {'shard'}, dimensions={0}, use_global_device_ids=true | all-gather | bytes 557056 | tf_op jit(solution)/shard_map/all_gather | solution.py:45
  175.5 0.2 reshape.41
  175.8 12.4 %maximum_select_fusion.2 = bf16[1024,4096]{1,0:T(8,128)(2,1)} fusion(bf16[512,4096]{1,0:T(8,128)(2,1)} %collective-permute-done.2, bf16[512,4096]{1,0:T(8,128)(2,1)} %maximum_select_fusion.3, pred[]{:T(512)S(6)} %eq.62), kind=kLoop, calls=%fused_computation.37 | loop fusion | flops 37748736 | bytes 16777216 | tf_op jit(solution)/shard_map/jit(_where)/select_n | solution.py:19
  188.2 4.6 select_add_fusion
  192.8 639.5 %while.17 = (s32[]{:T(128)}, f32[512,4096]{1,0:T(8,128)}, s32[]{:T(128)}, s32[4096]{0:T(1024)S(1)}, s32[]{:T(128)}, /*index=5*/s32[]{:T(128)}, s32[]{:T(128)}, s...) while((s32[]{:T(128)}, f32[512,4096]{1,0:T(8,128)}, ...), condition=%wide.region_6.7_spmd.clone, body=%wide.region_0.6_spmd.clone.sunk | while | flops 4838440960 | bytes 122046224 | solution.py:82
  192.8 1.7 dynamic-slice_select_fusion.6
  194.6 3.1 dynamic-slice_select_fusion.7
  197.7 21.7 %all-reduce.6.cloned.1.call-done = f32[512,128]{1,0:T(8,128)} async-done(((f32[512,128]{1,0:T(8,128)}), f32[512,128]{1,0:T(8,128)}) %all-reduce.6.cloned.1.call-update) | async-done | bytes 262160 | tf_op jit(solution)/shard_map/while/body/eval_jaxpr/psum | solution.py:26
  219.4 1.5 dynamic-slice_select_fusion.8
  221.0 397.9 %all-reduce.8.cloned.1.call-done = (f32[128,4096]{1,0:T(8,128)}, f32[128,128]{1,0:T(8,128)}) async-done(((f32[128,4096]{1,0:T(8,128)}, f32[128,128]{1,0:T(8,128)}), (f32[128,4096]{1,0:T(8,128)}, f32[128,128]{1,0:T(8,128)})) %all-reduce.8.cloned.1.call-update) | async-done | bytes 2162704 | tf_op jit(solution)/shard_map/while/body/eval_jaxpr/psum | solution.py:26
  618.9 0.9 copy.9
  619.8 0.9 fusion.51
  620.7 11.7 %cholesky.59 = f32[128,128]{1,0:T(8,128)S(1)} custom-call(f32[128,128]{1,0:T(8,128)S(1)} %fusion.51), custom_call_target="Cholesky" | custom-call | tf_op jit(solution)/shard_map/while/body/eval_jaxpr/jit(cholesky)/cholesky | solution.py:30
  632.4 0.6 compare_reduce_fusion.2
  633.1 0.7 fusion.52
  633.7 9.8 %custom-call.26 = f32[1,128,128]{1,2,0:T(8,128)S(1)} custom-call(f32[1,128,128]{2,1,0:T(8,128)S(1)} %fusion.52), custom_call_target="InvertDiagBlocksLowerTriangular" | custom-call | tf_op jit(solution)/shard_map/while/body/eval_jaxpr/triangular_solve | solution.py:32
  643.6 3.7 fusion.53
  647.3 1.9 fusion.54
  649.2 8.3 convolution_subtract_fusion.2
  657.5 0.4 add_dynamic-update-slice_fusion.2
  657.9 3.4 copy-done.1
  661.3 1.7 dynamic-slice_select_fusion.6
  663.0 0.0 all-reduce.8.cloned.1.call-start
  663.1 3.1 dynamic-slice_select_fusion.7
  666.2 20.7 %all-reduce.6.cloned.1.call-done = f32[512,128]{1,0:T(8,128)} async-done(((f32[512,128]{1,0:T(8,128)}), f32[512,128]{1,0:T(8,128)}) %all-reduce.6.cloned.1.call-update) | async-done | bytes 262160 | tf_op jit(solution)/shard_map/while/body/eval_jaxpr/psum | solution.py:26
  687.0 1.5 dynamic-slice_select_fusion.8
  688.5 101.3 %all-reduce.8.cloned.1.call-done = (f32[128,4096]{1,0:T(8,128)}, f32[128,128]{1,0:T(8,128)}) async-done(((f32[128,4096]{1,0:T(8,128)}, f32[128,128]{1,0:T(8,128)}), (f32[128,4096]{1,0:T(8,128)}, f32[128,128]{1,0:T(8,128)})) %all-reduce.8.cloned.1.call-update) | async-done | bytes 2162704 | tf_op jit(solution)/shard_map/while/body/eval_jaxpr/psum | solution.py:26
  789.8 0.9 copy.9
  790.8 0.9 fusion.51
  791.6 11.7 %cholesky.59 = f32[128,128]{1,0:T(8,128)S(1)} custom-call(f32[128,128]{1,0:T(8,128)S(1)} %fusion.51), custom_call_target="Cholesky" | custom-call | tf_op jit(solution)/shard_map/while/body/eval_jaxpr/jit(cholesky)/cholesky | solution.py:30
  803.4 0.6 compare_reduce_fusion.2
  804.0 0.7 fusion.52
  804.7 9.8 %custom-call.26 = f32[1,128,128]{1,2,0:T(8,128)S(1)} custom-call(f32[1,128,128]{2,1,0:T(8,128)S(1)} %fusion.52), custom_call_target="InvertDiagBlocksLowerTriangular" | custom-call | tf_op jit(solution)/shard_map/while/body/eval_jaxpr/triangular_solve | solution.py:32
  814.5 3.7 fusion.53
  818.3 1.9 fusion.54
  820.2 8.3 convolution_subtract_fusion.2
  828.5 0.4 add_dynamic-update-slice_fusion.2
  828.9 3.4 copy-done.1
  832.3 18.2 %fusion.20 = f32[512,2048]{1,0:T(8,128)} fusion(bf16[1024,4096]{1,0:T(8,128)(2,1)} %collective-permute-done.3, bf16[1024,4096]{1,0:T(8,128)(2,1)} %maximum_select_fusion.2, pred[]{:T(512)S(6)} %eq.61, f32[512,4096]{1,0:T(8,128)} %get-tuple-element.154), kind=kOutput, calls=%fused_computation.30 | convolution fusion | flops 8667529216 | bytes 29360128 | tf_op jit(solution)/shard_map/dot_general | solution.py:84
  850.5 53.1 %reduce-scatter.2.cloned.1.call-done = f32[512,1024]{1,0:T(8,128)} async-done(((f32[512,2048]{1,0:T(8,128)}), f32[512,1024]{1,0:T(8,128)}) %reduce-scatter.2.cloned.1.call-update) | async-done | bytes 2097168 | tf_op jit(solution)/shard_map/reduce_scatter | solution.py:90
  903.6 2.7 convert_element_type.7
  (33 shorter events, 0.3 us)
Async XLA Ops:
  8.0 61.4 %copy-start.3 = (bf16[2,8192]{1,0:T(2,128)(2,1)S(1)}, bf16[2,8192]{1,0:T(2,128)(2,1)}, u32[]{:S(2)}) copy-start(bf16[2,8192]{1,0:T(2,128)(2,1)} %param.6) | copy-start | bytes 98308
  8.0 3.1 collective-permute-start
  13.3 49.0 %collective-permute-start.1 = (bf16[256,4096]{1,0:T(8,128)(2,1)S(1)}, bf16[256,4096]{1,0:T(8,128)(2,1)}, u32[]{:S(2)}, u32[]{:S(2)}) collective-permute-start(bf16[256,4096]{1,0:T(8,128)(2,1)S(1)} %maximum_select_fusion.4), channel_id=1, source_target_pairs={{0,2},{1,3},{2,0},{3,1},{4,6},{5,7},{6,4},{7,5},{8,10},{9,11},{10,... | collective-permute-start | bytes 6291464 | tf_op jit(solution)/shard_map/ppermute | solution.py:16
  67.0 108.8 %collective-permute-start.2 = (bf16[512,4096]{1,0:T(8,128)(2,1)}, bf16[512,4096]{1,0:T(8,128)(2,1)}, u32[]{:S(2)}, u32[]{:S(2)}) collective-permute-start(bf16[512,4096]{1,0:T(8,128)(2,1)} %maximum_select_fusion.3), channel_id=1, source_target_pairs={{0,4},{1,5},{2,6},{3,7},{4,0},{5,1},{6,2},{7,3},{8,12},{9,13},{10,... | collective-permute-start | bytes 12582920 | tf_op jit(solution)/shard_map/ppermute | solution.py:16
  175.7 12.4 %slice-start = ((s8[8388608]{0:T(1024)(128)(4,1)}), s8[4194304]{0:T(1024)(128)(4,1)S(1)}, s32[]{:S(2)}) async-start(s8[8388608]{0:T(1024)(128)(4,1)} %bitcast.31), calls=%async_computation.4 | async-start | bytes 8388608
  175.7 12.4 %slice-start.1 = ((s8[8388608]{0:T(1024)(128)(4,1)}), s8[4194304]{0:T(1024)(128)(4,1)S(1)}, s32[]{:S(2)}) async-start(s8[8388608]{0:T(1024)(128)(4,1)} %bitcast.31), calls=%async_computation.5 | async-start | bytes 8388608
  188.2 644.1 %collective-permute-start.3 = (bf16[1024,4096]{1,0:T(8,128)(2,1)}, bf16[1024,4096]{1,0:T(8,128)(2,1)}, u32[]{:S(2)}, u32[]{:S(2)}) collective-permute-start(bf16[1024,4096]{1,0:T(8,128)(2,1)} %maximum_select_fusion.2), channel_id=1, source_target_pairs={{0,8},{1,9},{2,10},{3,11},{4,12},{5,13},{6,14},{7,15},{8,0},{9,1},... | collective-permute-start | bytes 25165832 | tf_op jit(solution)/shard_map/ppermute | solution.py:16
  192.8 26.6 %all-reduce.6.cloned.1.call-start = ((), (), s32[]{:S(2)}) async-start(), calls=%async_computation.2 | async-start | bytes 524288 | tf_op jit(solution)/shard_map/while/body/eval_jaxpr/psum | solution.py:26
  194.5 424.4 %all-reduce.8.cloned.1.call-start = ((), (), s32[]{:S(2)}) async-start(), calls=%async_computation.3 | async-start | bytes 4325376 | tf_op jit(solution)/shard_map/while/body/eval_jaxpr/psum | solution.py:26
  219.4 429.8 %copy-start.2 = (f32[512,128]{1,0:T(8,128)S(1)}, f32[512,128]{1,0:T(8,128)}, u32[]{:S(2)}) copy-start(f32[512,128]{1,0:T(8,128)} %all-reduce.6.cloned.1.call-done) | copy-start | bytes 786436 | tf_op jit(solution)/shard_map/while
  643.6 5.7 copy-start
  657.9 3.4 copy-start.1
  661.3 25.6 %all-reduce.6.cloned.1.call-start = ((), (), s32[]{:S(2)}) async-start(), calls=%async_computation.2 | async-start | bytes 524288 | tf_op jit(solution)/shard_map/while/body/eval_jaxpr/psum | solution.py:26
  663.0 126.8 %all-reduce.8.cloned.1.call-start = ((), (), s32[]{:S(2)}) async-start(), calls=%async_computation.3 | async-start | bytes 4325376 | tf_op jit(solution)/shard_map/while/body/eval_jaxpr/psum | solution.py:26
  687.0 133.2 %copy-start.2 = (f32[512,128]{1,0:T(8,128)S(1)}, f32[512,128]{1,0:T(8,128)}, u32[]{:S(2)}) copy-start(f32[512,128]{1,0:T(8,128)} %all-reduce.6.cloned.1.call-done) | copy-start | bytes 786436 | tf_op jit(solution)/shard_map/while
  814.5 5.7 copy-start
  828.9 3.4 copy-start.1
  832.3 71.3 %reduce-scatter.2.cloned.1.call-start = ((), (), s32[]{:S(2)}) async-start(), calls=%async_computation.1 | async-start | bytes 6291456 | tf_op jit(solution)/shard_map/reduce_scatter | solution.py:90
Sparse Core Ops, SparseCore 0:
  196.4 22.9 all-reduce.5
  223.6 395.2 all-reduce.7
  665.0 21.9 all-reduce.5
  691.0 98.8 all-reduce.7
Sparse Core Ops, SparseCore 1:
  850.6 53.0 reduce-scatter.1
